TPU v7x, 32 devices: a whole 2x2x4 slice. The times are simulated.
32 devices in a mesh: dom: 2 (over x), ty: 4 (over y, core), tx: 4 (over z).
Axes of the slice: x: 2, y: 2, z: 4, core: 2. Of those that a mesh axis runs over, the one named last changes fastest.
Arguments:
- state: float32 [5, 4, 256, 512], P(None, None, ('dom', 'ty'), 'tx')
- vert_mix: float32 [256, 512], P(('dom', 'ty'), 'tx'), may hold values from 0.1 to 2
- fb_mask: int32 [256, 512], P(('dom', 'ty'), 'tx'), may hold values 0 or 1
- nu_coef: float32 [4, 5, 4], replicated, may hold values from 0.04 to 0.18
- adv_coef: float32 [4, 5, 4], replicated, may hold values from 0.05 to 0.2
- anchors: int32 [3, 2], replicated, may hold values from 0 to 256, as said below
Outputs:
- new_state: float32 [5, 4, 256, 512], P(None, None, ('dom', 'ty'), 'tx')
Inputs may be any that keep to these rules, and one draw needn't show every extreme that they name: anchors[k] is the parent cell (row, column) where nest k+1's footprint of 32 x 512/2 parent cells begins; rows are multiples of 32, columns multiples of 128 up to 256; nest 1's row lies from 32 to 32, nests 2 and 3 take rows 0 and 32 in some order; column 0 and column 256 each occur in every draw; footprints may intersect.
All inputs are finite; a program needn't handle non-finite values. No bound on the sum of `fb_mask` on one device may be relied on, other than what follows from the above.
Results may differ from a plain program's by a relative error of at most 0.0003.
Values sent between devices are 32-bit elements; how exact they have to be, the bound alone decides.
A program may use at most 128 MiB of HBM per device.

v0:
```python
import functools

import jax
import jax.numpy as jnp
from jax import lax
from jax.experimental import pallas as pl
from jax.experimental.pallas import tpu as pltpu
from jax.sharding import PartitionSpec as P

SUBSTEPS = 3
MESH = pl.DeviceIdType.MESH


def repeat(count, body):
    if count <= 4:
        for index in range(count):
            body(index)
    else:

        def step(index, carry):
            body(index)
            return carry

        lax.fori_loop(0, count, step, 0)


def kernel(
    row_tiles,
    col_tiles,
    whole,
    mix,
    mask,
    nu,
    adv,
    anchors,
    out,
    state,
    current,
    packs,
    halo_rows,
    halo_cols,
    old_rows,
    new_rows,
    old_cols,
    new_cols,
    spread_rows,
    spread_cols,
    ghost_rows,
    ghost_cols,
    coef,
    piece,
    swapped,
    chosen,
    one_sums,
    slot_sums,
    load_sem,
    halo_send,
    halo_recv,
    edge_send,
    edge_recv,
    swap_sem,
    feed_send,
    one_recv,
    slot_recv,
):
    nfield, nlevel, nrow, ncol = state.shape
    count = nfield * nlevel
    padded = packs.shape[1] - nrow
    padded = padded // 2
    half = count // 2
    edge_rows, edge_cols = (old_rows, new_rows), (old_cols, new_cols)
    hrow, hcol = nrow // 2, ncol // 2
    half_rows = row_tiles // 2
    foot = half_rows // 2
    span = col_tiles // 2
    places = span + 1

    dom = lax.axis_index("dom")
    ty = lax.axis_index("ty")
    j = lax.axis_index("tx")
    parity = ty % 2
    i = ty // 2
    domain = 2 * dom + parity
    is_parent = domain == 0
    is_nest = domain > 0
    row_id = lax.broadcasted_iota(jnp.int32, (nrow, ncol), 0)
    lane = lax.broadcasted_iota(jnp.int32, (nrow, ncol), 1)

    def device(number, row, col):
        return (number // 2, 2 * row + number % 2, col)

    def copy(src, dst, send, recv, target):
        return pltpu.make_async_remote_copy(
            src_ref=src,
            dst_ref=dst,
            send_sem=send,
            recv_sem=recv,
            device_id=target,
            device_id_type=MESH,
        )

    fetch = pltpu.make_async_copy(whole, state, load_sem)
    fetch.start()
    barrier = pltpu.get_barrier_semaphore()

    def greet(target):
        pl.semaphore_signal(barrier, inc=1, device_id=target, device_id_type=MESH)

    greeted = jnp.int32(0)
    for there, row, col in (
        (i > 0, i - 1, j),
        (i < half_rows - 1, i + 1, j),
        (j > 0, i, j - 1),
        (j < col_tiles - 1, i, j + 1),
    ):
        greeted = greeted + there.astype(jnp.int32)

        @pl.when(there)
        def _():
            greet(device(domain, row, col))

    @pl.when(is_parent)
    def _():
        def nests(number, row_start, back):
            row_gap = i - row_start
            place = j - back

            @pl.when((row_gap >= 0) & (row_gap < foot) & (place >= 0) & (place < places))
            def _():
                for p in range(2):
                    for q in range(2):
                        greet(device(number, 2 * row_gap + p, 2 * back + q))

        for number in (2, 3):
            repeat(span, lambda back, number=number: nests(number, (i // foot) * foot, back))
        repeat(foot * span, lambda flat: nests(1, 1 + flat // span, flat % span))

    @pl.when(domain == 1)
    def _():
        repeat(
            foot * places,
            lambda flat: greet(
                device(0, 1 + flat // places + i // 2, flat % places + j // 2)
            ),
        )

    @pl.when(domain > 1)
    def _():
        greet((dom, 2 * i + 1 - parity, j))
        repeat(
            2 * places,
            lambda flat: greet(
                device(0, flat // places * foot + i // 2, flat % places + j // 2)
            ),
        )

    def pack(load, phase):
        packed = jnp.zeros((nrow, ncol), jnp.float32)
        for k in range(count):
            cells = load(k // nlevel, k % nlevel)
            packs[phase, k : k + 1, :] = cells[0:1, :]
            packs[phase, padded + k : padded + k + 1, :] = cells[nrow - 1 : nrow, :]
            rolled = pltpu.roll(cells, 2 * k + 1, 1)
            packed = jnp.where((lane == 2 * k) | (lane == 2 * k + 1), rolled, packed)
        if padded > count:
            rest = jnp.zeros((padded - count, ncol), jnp.float32)
            packs[phase, count:padded, :] = rest
            packs[phase, padded + count : 2 * padded, :] = rest
        packs[phase, 2 * padded :, :] = packed

    first_row = pl.ds(0, padded)
    last_row = pl.ds(padded, padded)
    side_cols = pl.ds(2 * padded, nrow)

    def halo(phase, act):
        moves = (
            (0, i < half_rows - 1, last_row, halo_rows, 0, i + 1, j, i > 0, i - 1, j),
            (1, i > 0, first_row, halo_rows, 1, i - 1, j, i < half_rows - 1, i + 1, j),
            (2, j < col_tiles - 1, side_cols, halo_cols, 0, i, j + 1, j > 0, i, j - 1),
            (3, j > 0, side_cols, halo_cols, 1, i, j - 1, j < col_tiles - 1, i, j + 1),
        )
        for way, sends, rows, buffer, side, row, col, takes, from_row, from_col in moves:

            def transfer(target, rows=rows, buffer=buffer, side=side, way=way):
                return copy(
                    packs.at[phase, rows],
                    buffer.at[phase, side],
                    halo_send.at[phase, way],
                    halo_recv.at[phase, way],
                    target,
                )

            if act == "start":

                @pl.when(sends)
                def _():
                    transfer(device(domain, row, col)).start()

            elif act == "recv":

                @pl.when(takes)
                def _():
                    transfer(device(domain, from_row, from_col)).wait_recv()

            else:

                @pl.when(sends)
                def _():
                    transfer(device(domain, row, col)).wait_send()

    def edges_out(phase, act):
        def one(number, option, row_start, back, index):
            row_gap = i - row_start
            place = j - back
            fits = (row_gap >= 0) & (row_gap < foot) & (place >= 0) & (place < places)
            slot = option * places + place
            for p in range(2):
                for q in range(2):
                    row = 2 * row_gap + p
                    col = 2 * back + q
                    target = device(number, row, col)
                    spot = 4 * index + 2 * p + q

                    def rows_copy(source):
                        return copy(
                            packs.at[phase, source],
                            edge_rows[phase].at[slot],
                            edge_send.at[phase, 0, spot],
                            edge_recv.at[phase, 0, slot],
                            target,
                        )

                    def cols_copy():
                        return copy(
                            packs.at[phase, pl.ds(2 * padded + p * hrow, hrow)],
                            edge_cols[phase].at[slot],
                            edge_send.at[phase, 1, spot],
                            edge_recv.at[phase, 1, slot],
                            target,
                        )

                    def go(transfer):
                        if act == "start":
                            transfer.start()
                        else:
                            transfer.wait_send()

                    @pl.when(fits & ((col == 0) | (col == col_tiles - 1)))
                    def _():
                        go(cols_copy())

                    @pl.when(fits & (row == 0))
                    def _():
                        go(rows_copy(first_row))

                    @pl.when(fits & (row == half_rows - 1))
                    def _():
                        go(rows_copy(last_row))

        for number in (2, 3):
            option = i // foot
            base = (number - 2) * span
            repeat(
                span,
                lambda back, number=number, option=option, base=base: one(
                    number, option, option * foot, back, base + back
                ),
            )

        def nest_one(flat):
            option = flat // span
            back = flat % span
            one(1, option, 1 + option, back, 2 * span + flat)

        repeat(foot * span, nest_one)

    at_row_end = (i == 0) | (i == half_rows - 1)
    at_col_end = (j == 0) | (j == col_tiles - 1)
    number_here = jnp.maximum(domain - 1, 0)
    row_here = anchors[0, number_here] // nrow
    col_here = anchors[1, number_here] // ncol
    option_here = jnp.where(domain == 1, row_here - 1, row_here // foot)
    slot_here = jnp.clip(option_here * places + col_here, 0, old_rows.shape[0] - 1)

    def edges_in(phase):
        def wait(slot):
            away = device(0, i // 2, j // 2)

            @pl.when(at_row_end)
            def _():
                copy(
                    packs.at[phase, first_row],
                    edge_rows[phase].at[slot],
                    edge_send.at[phase, 0, 0],
                    edge_recv.at[phase, 0, slot],
                    away,
                ).wait_recv()

            @pl.when(at_col_end)
            def _():
                copy(
                    packs.at[phase, pl.ds(2 * padded, hrow)],
                    edge_cols[phase].at[slot],
                    edge_send.at[phase, 1, 0],
                    edge_recv.at[phase, 1, slot],
                    away,
                ).wait_recv()

        @pl.when(domain == 1)
        def _():
            repeat(foot * places, wait)

        @pl.when(domain > 1)
        def _():
            repeat(2 * places, wait)

        @pl.when(at_row_end)
        def _():
            source = lax.broadcasted_iota(jnp.int32, (ncol, ncol), 0)
            target = lax.broadcasted_iota(jnp.int32, (ncol, ncol), 1)
            spread = (source == (j % 2) * hcol + target // 2).astype(jnp.float32)
            spread_rows[phase] = jnp.dot(
                edge_rows[phase][slot_here],
                spread,
                precision=lax.Precision.HIGHEST,
                preferred_element_type=jnp.float32,
            )

        @pl.when(at_col_end)
        def _():
            values = edge_cols[phase][slot_here]
            spread_cols[phase, pl.ds(0, hrow, stride=2), :] = values
            spread_cols[phase, pl.ds(1, hrow, stride=2), :] = values

    def ghosts(phase):
        def blended(values):
            if phase == 0:
                return values[0]
            return values[0] + (phase / SUBSTEPS) * (values[1] - values[0])

        for side, inner in ((0, i > 0), (1, i < half_rows - 1)):

            @pl.when(inner)
            def _():
                ghost_rows[side] = halo_rows[phase, side]

            @pl.when(jnp.logical_not(inner) & is_nest)
            def _():
                ghost_rows[side] = blended(spread_rows)

            @pl.when(jnp.logical_not(inner) & is_parent)
            def _():
                ghost_rows[side] = jnp.zeros((padded, ncol), jnp.float32)

        for side, inner in ((0, j > 0), (1, j < col_tiles - 1)):

            @pl.when(inner)
            def _():
                ghost_cols[side] = halo_cols[phase, side]

            @pl.when(jnp.logical_not(inner) & is_nest)
            def _():
                shift = ncol - 1 if side == 0 else 1
                ghost_cols[side] = pltpu.roll(blended(spread_cols), shift, 1)

            @pl.when(jnp.logical_not(inner) & is_parent)
            def _():
                ghost_cols[side] = jnp.zeros((nrow, ncol), jnp.float32)

    def advance(load, store):
        sides = jnp.where(lane % 2 == 0, ghost_cols[0], ghost_cols[1])
        mixing = mix[...]
        for f in range(nfield):
            forward = []
            for level in range(nlevel):
                k = f * nlevel + level
                cells = load(f, level)
                diffusion = nu[domain, level, f]
                advection = adv[domain, level, f]
                above = jnp.where(
                    row_id == 0, ghost_rows[0, k : k + 1, :], pltpu.roll(cells, 1, 0)
                )
                below = jnp.where(
                    row_id == nrow - 1,
                    ghost_rows[1, k : k + 1, :],
                    pltpu.roll(cells, nrow - 1, 0),
                )
                beside = pltpu.roll(sides, (ncol - 2 * k - 1) % ncol, 1)
                west = pltpu.roll(jnp.where(lane == ncol - 1, beside, cells), 1, 1)
                east = pltpu.roll(jnp.where(lane == 0, beside, cells), ncol - 1, 1)
                explicit = (
                    cells
                    + diffusion * (above + below + west + east - 4.0 * cells)
                    + advection * (west - cells)
                )
                if level == 0:
                    forward.append(explicit * coef[level])
                else:
                    forward.append((explicit + mixing * forward[-1]) * coef[level])
            solved = forward[-1]
            store(f, nlevel - 1, solved)
            for level in range(nlevel - 2, -1, -1):
                solved = forward[level] + coef[nlevel + level] * solved
                store(f, level, solved)

    def put(buffer, *prefix):
        def store(f, level, values):
            buffer[(*prefix, f, level)] = values

        return store

    def get(buffer, *prefix):
        return lambda f, level: buffer[(*prefix, f, level)]

    mixing = mix[...]
    ratio = None
    for level in range(nlevel):
        ends = (1.0 if level == 0 else 0.0) + (1.0 if level == nlevel - 1 else 0.0)
        pivot = 1.0 + mixing * (2.0 - ends)
        if level > 0:
            pivot = pivot - mixing * ratio
        inverse = 1.0 / pivot
        ratio = mixing * inverse
        coef[level] = inverse
        coef[nlevel + level] = ratio

    fetch.wait()
    pack(get(state), 0)
    backs = jnp.minimum(span - 1, j) - jnp.maximum(0, j - span) + 1
    gaps = jnp.minimum(foot - 1, i - 1) - jnp.maximum(0, i - foot) + 1
    partners = jnp.where(
        is_parent,
        4 * backs * (2 + gaps),
        jnp.where(domain == 1, foot * places, 1 + 2 * places),
    )
    pl.semaphore_wait(barrier, greeted + partners)
    halo(0, "start")

    @pl.when(is_parent)
    def _():
        edges_out(0, "start")

    halo(0, "recv")

    @pl.when(is_nest)
    def _():
        edges_in(0)

    ghosts(0)
    advance(get(state), put(current, 0))
    pack(get(current, 0), 1)

    @pl.when(is_parent)
    def _():
        edges_out(1, "start")

    feeds = foot * places

    def feed_one(flat):
        option = flat // places
        place = flat % places
        where_to = device(0, 1 + option + i // 2, place + j // 2)
        part = 2 * (i % 2) + j % 2
        return copy(
            chosen,
            one_sums.at[flat, part],
            feed_send.at[flat],
            one_recv.at[flat, part],
            where_to,
        )

    def feed_slot(place):
        where_to = device(0, parity * foot + i // 2, place + j // 2)
        part = 2 * (i % 2) + j % 2
        return copy(
            chosen,
            slot_sums.at[place, part],
            feed_send.at[place],
            slot_recv.at[place, part],
            where_to,
        )

    def swap():
        return copy(
            piece, swapped, swap_sem.at[0], swap_sem.at[1], (dom, 2 * i + 1 - parity, j)
        )

    @pl.when(is_nest)
    def _():
        halo(1, "start")
        halo(1, "recv")
        edges_in(1)
        ghosts(1)
        advance(get(current, 0), put(current, 1))
        pack(get(current, 1), 2)
        halo(2, "start")
        halo(2, "recv")
        ghosts(2)
        advance(get(current, 1), put(out))
        source = lax.broadcasted_iota(jnp.int32, (2 * ncol, ncol), 0)
        target = lax.broadcasted_iota(jnp.int32, (2 * ncol, ncol), 1)
        gather = (target == source // 2).astype(jnp.float32)
        even = mask[pl.ds(0, hrow, stride=2), :].astype(jnp.float32)
        odd = mask[pl.ds(1, hrow, stride=2), :].astype(jnp.float32)

        def pairs(k):
            f, level = k // nlevel, k % nlevel
            return (
                even * out[f, level, pl.ds(0, hrow, stride=2), :]
                + odd * out[f, level, pl.ds(1, hrow, stride=2), :]
            )

        tall = []
        for k in range(half):
            tall.append(jnp.concatenate([pairs(k), pairs(k + half)], axis=1))
        tall.append(jnp.concatenate([even + odd, jnp.zeros_like(even)], axis=1))
        piece[...] = jnp.dot(
            jnp.concatenate(tall, axis=0),
            gather,
            precision=lax.Precision.HIGHEST,
            preferred_element_type=jnp.float32,
        )

        @pl.when(domain == 1)
        def _():
            chosen[...] = piece[...]
            repeat(feeds, lambda flat: feed_one(flat).start())

        @pl.when(domain > 1)
        def _():
            swap().start()
            swap().wait_recv()
            mine = row_here == parity * foot
            chosen[...] = jnp.where(mine, piece[...], swapped[...])
            repeat(places, lambda place: feed_slot(place).start())

    @pl.when(is_parent)
    def _():
        away = device(1, i // 2, j // 2)

        def take_one(flat):
            option = flat // places
            place = flat % places
            row_gap = i - 1 - option
            back = j - place

            @pl.when((row_gap >= 0) & (row_gap < foot) & (back >= 0) & (back < span))
            def _():
                for part in range(4):
                    copy(
                        chosen,
                        one_sums.at[flat, part],
                        feed_send.at[0],
                        one_recv.at[flat, part],
                        away,
                    ).wait_recv()

        def take_slot(place):
            back = j - place

            @pl.when((back >= 0) & (back < span))
            def _():
                for part in range(4):
                    copy(
                        chosen,
                        slot_sums.at[place, part],
                        feed_send.at[0],
                        slot_recv.at[place, part],
                        away,
                    ).wait_recv()

        repeat(feeds, take_one)
        repeat(places, take_slot)
        one_row = anchors[0, 0] // nrow
        one_col = anchors[1, 0] // ncol
        slot = i // foot
        second = anchors[0, 1] // nrow == slot * foot
        slot_col = jnp.where(second, anchors[1, 1], anchors[1, 2]) // ncol
        slot_at = jnp.clip(slot_col, 0, places - 1)
        one_in = (i >= one_row) & (i < one_row + foot) & (j >= one_col) & (j < one_col + span)
        slot_in = (j >= slot_col) & (j < slot_col + span)
        one_at = jnp.clip((one_row - 1) * places + one_col, 0, feeds - 1)
        left = lax.broadcasted_iota(jnp.int32, (hrow, ncol), 1) < hcol

        def both(part, rows):
            one = one_sums[one_at, part, rows, :]
            other = slot_sums[slot_at, part, rows, :]
            return jnp.where(one_in, one, 0.0) + jnp.where(slot_in, other, 0.0)

        for p in range(2):
            here = slice(p * hrow, (p + 1) * hrow)
            rows = slice(half * hrow, (half + 1) * hrow)
            total = jnp.where(
                left, both(2 * p, rows), pltpu.roll(both(2 * p + 1, rows), hcol, 1)
            )
            accept = (mask[here, :] == 1) & (total > 0.0)
            scale = 1.0 / jnp.maximum(total, 1.0)
            for k in range(half):
                rows = slice(k * hrow, (k + 1) * hrow)
                near = both(2 * p, rows)
                far = both(2 * p + 1, rows)
                low = jnp.where(left, near, pltpu.roll(far, hcol, 1))
                high = jnp.where(left, pltpu.roll(near, hcol, 1), far)
                for field, sums in ((k, low), (k + half, high)):
                    f, level = field // nlevel, field % nlevel
                    out[f, level, here, :] = jnp.where(
                        accept, sums * scale, current[0, f, level, here, :]
                    )

    halo(0, "send")

    @pl.when(is_parent)
    def _():
        edges_out(0, "send")
        edges_out(1, "send")

    @pl.when(is_nest)
    def _():
        halo(1, "send")
        halo(2, "send")

        @pl.when(domain == 1)
        def _():
            repeat(feeds, lambda flat: feed_one(flat).wait_send())

        @pl.when(domain > 1)
        def _():
            swap().wait_send()
            repeat(places, lambda place: feed_slot(place).wait_send())


def shards(row_tiles, col_tiles, state, vert_mix, fb_mask, nu_coef, adv_coef, anchors):
    nfield, nlevel, nrow, ncol = state.shape
    count = nfield * nlevel
    padded = -(-count // 8) * 8
    foot = row_tiles // 4
    span = col_tiles // 2
    places = span + 1
    options = max(foot, 2)
    tall = (count // 2 + 1) * (nrow // 2)
    sent = 4 * (2 * span + foot * span)
    f32 = jnp.float32
    vmem = pl.BlockSpec(memory_space=pltpu.VMEM)
    smem = pl.BlockSpec(memory_space=pltpu.SMEM)
    dma = pltpu.SemaphoreType.DMA
    return pl.pallas_call(
        functools.partial(kernel, row_tiles, col_tiles),
        out_shape=jax.ShapeDtypeStruct(state.shape, f32),
        in_specs=[pl.BlockSpec(memory_space=pl.ANY), vmem, vmem, smem, smem, smem],
        out_specs=vmem,
        scratch_shapes=[
            pltpu.VMEM(state.shape, f32),
            pltpu.VMEM((2, nfield, nlevel, nrow, ncol), f32),
            pltpu.VMEM((3, 2 * padded + nrow, ncol), f32),
            pltpu.VMEM((3, 2, padded, ncol), f32),
            pltpu.VMEM((3, 2, nrow, ncol), f32),
            pltpu.VMEM((options * places, padded, ncol), f32),
            pltpu.VMEM((options * places, padded, ncol), f32),
            pltpu.VMEM((options * places, nrow // 2, ncol), f32),
            pltpu.VMEM((options * places, nrow // 2, ncol), f32),
            pltpu.VMEM((2, padded, ncol), f32),
            pltpu.VMEM((2, nrow, ncol), f32),
            pltpu.VMEM((2, padded, ncol), f32),
            pltpu.VMEM((2, nrow, ncol), f32),
            pltpu.VMEM((2 * nlevel, nrow, ncol), f32),
            pltpu.VMEM((tall, ncol), f32),
            pltpu.VMEM((tall, ncol), f32),
            pltpu.VMEM((tall, ncol), f32),
            pltpu.VMEM((foot * places, 4, tall, ncol), f32),
            pltpu.VMEM((places, 4, tall, ncol), f32),
            dma,
            dma((3, 4)),
            dma((3, 4)),
            dma((2, 2, sent)),
            dma((2, 2, options * places)),
            dma((2,)),
            dma((foot * places,)),
            dma((foot * places, 4)),
            dma((places, 4)),
        ],
        compiler_params=pltpu.CompilerParams(has_side_effects=True, collective_id=0),
    )(
        state,
        vert_mix,
        fb_mask,
        jnp.swapaxes(nu_coef, 1, 2),
        jnp.swapaxes(adv_coef, 1, 2),
        jnp.swapaxes(anchors, 0, 1),
    )


def solution(mesh):
    in_specs = (
        P(None, None, ("dom", "ty"), "tx"),
        P(("dom", "ty"), "tx"),
        P(("dom", "ty"), "tx"),
        P(),
        P(),
        P(),
    )
    out_specs = P(None, None, ("dom", "ty"), "tx")
    body = functools.partial(shards, mesh.shape["ty"], mesh.shape["tx"])
    return jax.shard_map(body, mesh=mesh, in_specs=in_specs, out_specs=out_specs, check_vma=False)
```

profile of v0, /device:TPU:8, one launch (start us, length us, event | category | flops | bytes accessed | tf_op | source)
XLA Modules:
  0.0 34.6 jit_solution(10101122781180169200)
XLA Ops:
  0.0 32.9 %shard_map.64 = f32[5,4,32,128]{3,2,1,0:T(8,128)} custom-call(f32[5,4,32,128]{3,2,1,0:T(8,128)} %whole.1, f32[32,128]{1,0:T(8,128)} %mix.1, s32[32,128]{1,0:T(8,128)} %mask.1, f32[4,4,5]{2,1,0:T(4,128)} %bitcast.3, f32[4,4,5]{2,1,0:T(4,128)} %bitcast.4, s32[2,3]{1,0:T(2,128)} %bitcast.5), custom_call_target="tpu_custom_call" | custom-call | tf_op jit(solution)/shard_map/pallas_call | solution.py:646
  32.9 1.7 %copy.8 = f32[5,4,32,128]{3,2,1,0:T(8,128)} copy(f32[5,4,32,128]{3,2,1,0:T(8,128)} %shard_map.64) | data formatting | bytes 655360
where the time goes:
time: 34.8 us; the launch traced here: 34.6 us
  Pallas kernels  32.9 us (95%)
  local copies, waits for them, and re-layouts  1.72 us (5%)
    pallas_call x1, Pallas kernels, shards(): pl.pallas_call(functools.partial(kernel, row_tiles, col_tiles), out_shape...  32.9 us
    unnamed x1, local copies, waits for them, and re-layouts  1.72 us

commit v1 on v0

--- a/solution.py
+++ b/solution.py
@@ -8,6 +8,7 @@
 from jax.sharding import PartitionSpec as P
 
 SUBSTEPS = 3
+VMEM_LIMIT = 32 << 20
 MESH = pl.DeviceIdType.MESH
 
 
@@ -37,6 +38,7 @@
     state,
     current,
     packs,
+    held,
     halo_rows,
     halo_cols,
     old_rows,
@@ -56,6 +58,8 @@
     load_sem,
     halo_send,
     halo_recv,
+    tell_send,
+    held_recv,
     edge_send,
     edge_recv,
     swap_sem,
@@ -119,8 +123,23 @@
         def _():
             greet(device(domain, row, col))
 
+    inside = half_rows > 2 and col_tiles > 2
+
+    def greet_sources(row):
+        def one(place):
+            col = place + j // 2
+
+            @pl.when((row != i) | (col != j))
+            def _():
+                greet(device(domain, row, col))
+
+        repeat(places, one)
+
     @pl.when(is_parent)
     def _():
+        for number in (1, 2, 3):
+            greet(device(number, i, j))
+
         def nests(number, row_start, back):
             row_gap = i - row_start
             place = j - back
@@ -129,30 +148,29 @@
             def _():
                 for p in range(2):
                     for q in range(2):
-                        greet(device(number, 2 * row_gap + p, 2 * back + q))
-
-        for number in (2, 3):
-            repeat(span, lambda back, number=number: nests(number, (i // foot) * foot, back))
-        repeat(foot * span, lambda flat: nests(1, 1 + flat // span, flat % span))
+                        row, col = 2 * row_gap + p, 2 * back + q
+
+                        @pl.when(
+                            (row > 0) & (row < half_rows - 1) & (col > 0) & (col < col_tiles - 1)
+                        )
+                        def _():
+                            greet(device(number, row, col))
+
+        if inside:
+            for number in (2, 3):
+                repeat(span, lambda back, number=number: nests(number, (i // foot) * foot, back))
+            repeat(foot * span, lambda flat: nests(1, 1 + flat // span, flat % span))
 
     @pl.when(domain == 1)
     def _():
-        repeat(
-            foot * places,
-            lambda flat: greet(
-                device(0, 1 + flat // places + i // 2, flat % places + j // 2)
-            ),
-        )
+        greet(device(0, i, j))
+        repeat(foot, lambda option: greet_sources(1 + option + i // 2))
 
     @pl.when(domain > 1)
     def _():
+        greet(device(0, i, j))
         greet((dom, 2 * i + 1 - parity, j))
-        repeat(
-            2 * places,
-            lambda flat: greet(
-                device(0, flat // places * foot + i // 2, flat % places + j // 2)
-            ),
-        )
+        repeat(2, lambda option: greet_sources(option * foot + i // 2))
 
     def pack(load, phase):
         packed = jnp.zeros((nrow, ncol), jnp.float32)
@@ -208,8 +226,17 @@
                 def _():
                     transfer(device(domain, row, col)).wait_send()
 
+    def tell(phase, number):
+        return copy(
+            packs.at[phase],
+            held.at[phase],
+            tell_send.at[phase, number - 1],
+            held_recv.at[phase],
+            device(number, i, j),
+        )
+
     def edges_out(phase, act):
-        def one(number, option, row_start, back, index):
+        def one(option, row_start, back, index):
             row_gap = i - row_start
             place = j - back
             fits = (row_gap >= 0) & (row_gap < foot) & (place >= 0) & (place < places)
@@ -218,61 +245,58 @@
                 for q in range(2):
                     row = 2 * row_gap + p
                     col = 2 * back + q
-                    target = device(number, row, col)
+                    here = (row == i) & (col == j)
                     spot = 4 * index + 2 * p + q
 
-                    def rows_copy(source):
-                        return copy(
-                            packs.at[phase, source],
-                            edge_rows[phase].at[slot],
-                            edge_send.at[phase, 0, spot],
-                            edge_recv.at[phase, 0, slot],
-                            target,
+                    def go(rows, kind, buffer):
+                        away = copy(
+                            held.at[phase, rows],
+                            buffer[phase].at[slot],
+                            edge_send.at[phase, kind, spot],
+                            edge_recv.at[phase, kind, slot],
+                            device(domain, row, col),
                         )
 
-                    def cols_copy():
-                        return copy(
-                            packs.at[phase, pl.ds(2 * padded + p * hrow, hrow)],
-                            edge_cols[phase].at[slot],
-                            edge_send.at[phase, 1, spot],
-                            edge_recv.at[phase, 1, slot],
-                            target,
-                        )
-
-                    def go(transfer):
+                        @pl.when(jnp.logical_not(here))
+                        def _():
+                            if act == "start":
+                                away.start()
+                            else:
+                                away.wait_send()
+
                         if act == "start":
-                            transfer.start()
-                        else:
-                            transfer.wait_send()
+
+                            @pl.when(here)
+                            def _():
+                                pltpu.make_async_copy(
+                                    held.at[phase, rows],
+                                    buffer[phase].at[slot],
+                                    edge_recv.at[phase, kind, slot],
+                                ).start()
 
                     @pl.when(fits & ((col == 0) | (col == col_tiles - 1)))
                     def _():
-                        go(cols_copy())
+                        go(pl.ds(2 * padded + p * hrow, hrow), 1, edge_cols)
 
                     @pl.when(fits & (row == 0))
                     def _():
-                        go(rows_copy(first_row))
+                        go(first_row, 0, edge_rows)
 
                     @pl.when(fits & (row == half_rows - 1))
                     def _():
-                        go(rows_copy(last_row))
-
-        for number in (2, 3):
+                        go(last_row, 0, edge_rows)
+
+        @pl.when(domain > 1)
+        def _():
             option = i // foot
-            base = (number - 2) * span
+            repeat(span, lambda back: one(option, option * foot, back, back))
+
+        @pl.when(domain == 1)
+        def _():
             repeat(
-                span,
-                lambda back, number=number, option=option, base=base: one(
-                    number, option, option * foot, back, base + back
-                ),
+                foot * span,
+                lambda flat: one(flat // span, 1 + flat // span, flat % span, flat),
             )
-
-        def nest_one(flat):
-            option = flat // span
-            back = flat % span
-            one(1, option, 1 + option, back, 2 * span + flat)
-
-        repeat(foot * span, nest_one)
 
     at_row_end = (i == 0) | (i == half_rows - 1)
     at_col_end = (j == 0) | (j == col_tiles - 1)
@@ -428,22 +452,35 @@
     pack(get(state), 0)
     backs = jnp.minimum(span - 1, j) - jnp.maximum(0, j - span) + 1
     gaps = jnp.minimum(foot - 1, i - 1) - jnp.maximum(0, i - foot) + 1
-    partners = jnp.where(
-        is_parent,
-        4 * backs * (2 + gaps),
-        jnp.where(domain == 1, foot * places, 1 + 2 * places),
-    )
+    option_start = (i // foot) * foot
+    lone = jnp.where(domain == 1, i >= 1, option_start == i - i // 2).astype(jnp.int32)
+    targets = 4 * backs * jnp.where(domain == 1, gaps, 1) - lone
+    if inside:
+        deep = jnp.logical_not(at_row_end | at_col_end).astype(jnp.int32)
+        targets = targets + deep * places * jnp.where(domain == 1, foot, 2)
+    partners = jnp.where(is_parent, 3, 1 + targets + jnp.where(domain == 1, 0, 1))
     pl.semaphore_wait(barrier, greeted + partners)
+
+    def relay(phase):
+        tell(phase, 1).wait_recv()
+        edges_out(phase, "start")
+
+    @pl.when(is_parent)
+    def _():
+        for number in (1, 2, 3):
+            tell(0, number).start()
+
     halo(0, "start")
 
-    @pl.when(is_parent)
-    def _():
-        edges_out(0, "start")
+    @pl.when(is_nest)
+    def _():
+        relay(0)
 
     halo(0, "recv")
 
     @pl.when(is_nest)
     def _():
+        relay(1)
         edges_in(0)
 
     ghosts(0)
@@ -452,7 +489,8 @@
 
     @pl.when(is_parent)
     def _():
-        edges_out(1, "start")
+        for number in (1, 2, 3):
+            tell(1, number).start()
 
     feeds = foot * places
 
@@ -611,13 +649,16 @@
 
     @pl.when(is_parent)
     def _():
+        for phase in range(2):
+            for number in (1, 2, 3):
+                tell(phase, number).wait_send()
+
+    @pl.when(is_nest)
+    def _():
+        halo(1, "send")
+        halo(2, "send")
         edges_out(0, "send")
         edges_out(1, "send")
-
-    @pl.when(is_nest)
-    def _():
-        halo(1, "send")
-        halo(2, "send")
 
         @pl.when(domain == 1)
         def _():
@@ -638,7 +679,7 @@
     places = span + 1
     options = max(foot, 2)
     tall = (count // 2 + 1) * (nrow // 2)
-    sent = 4 * (2 * span + foot * span)
+    sent = 4 * foot * span
     f32 = jnp.float32
     vmem = pl.BlockSpec(memory_space=pltpu.VMEM)
     smem = pl.BlockSpec(memory_space=pltpu.SMEM)
@@ -646,12 +687,13 @@
     return pl.pallas_call(
         functools.partial(kernel, row_tiles, col_tiles),
         out_shape=jax.ShapeDtypeStruct(state.shape, f32),
-        in_specs=[pl.BlockSpec(memory_space=pl.ANY), vmem, vmem, smem, smem, smem],
+        in_specs=[pl.BlockSpec(memory_space=pltpu.HBM), vmem, vmem, smem, smem, smem],
         out_specs=vmem,
         scratch_shapes=[
             pltpu.VMEM(state.shape, f32),
             pltpu.VMEM((2, nfield, nlevel, nrow, ncol), f32),
             pltpu.VMEM((3, 2 * padded + nrow, ncol), f32),
+            pltpu.VMEM((2, 2 * padded + nrow, ncol), f32),
             pltpu.VMEM((3, 2, padded, ncol), f32),
             pltpu.VMEM((3, 2, nrow, ncol), f32),
             pltpu.VMEM((options * places, padded, ncol), f32),
@@ -671,6 +713,8 @@
             dma,
             dma((3, 4)),
             dma((3, 4)),
+            dma((2, 3)),
+            dma((2,)),
             dma((2, 2, sent)),
             dma((2, 2, options * places)),
             dma((2,)),
@@ -678,7 +722,9 @@
             dma((foot * places, 4)),
             dma((places, 4)),
         ],
-        compiler_params=pltpu.CompilerParams(has_side_effects=True, collective_id=0),
+        compiler_params=pltpu.CompilerParams(
+            has_side_effects=True, collective_id=0, vmem_limit_bytes=VMEM_LIMIT
+        ),
     )(
         state,
         vert_mix,

time: 34.8 us -> 37 us (1.063); the launches traced: 34.6 us -> 36.3 us
  local copies, waits for them, and re-layouts: 1.72 us -> 5.2 us
  Pallas kernels: 32.9 us -> 31.1 us
    unnamed x1 -> x13, local copies, waits for them, and re-layouts: 1.72 us -> 5.2 us
    pallas_call x1, Pallas kernels: 32.9 us -> 31.1 us  [shards(): pl.pallas_call(functools.partial(kernel, row_tiles, col_tiles), out_shape...]
where the time goes in v1:
time: 37 us; the launch traced here: 36.3 us
  Pallas kernels  31.1 us (84%)
  local copies, waits for them, and re-layouts  5.2 us (14%)
    pallas_call x1, Pallas kernels, shards(): pl.pallas_call(functools.partial(kernel, row_tiles, col_tiles), out_shape...  31.1 us
    unnamed x13, local copies, waits for them, and re-layouts  5.2 us

profile of v1, /device:TPU:8, one launch (start us, length us, event | category | flops | bytes accessed | tf_op | source)
XLA Modules:
  0.0 36.3 jit_solution(12976984955428943722)
XLA Ops:
  0.0 0.0 copy-start.5
  0.0 0.7 %copy-done.5 = s32[3,2]{0,1:T(2,128)S(1)} copy-done((s32[3,2]{0,1:T(2,128)S(1)}, s32[3,2]{0,1:T(2,128)}, u32[]{:S(2)}) %copy-start.5) | copy-done | bytes 48
  0.7 0.0 copy-start
  0.7 1.0 %copy-done = f32[5,4,32,128]{3,2,1,0:T(8,128)S(1)} copy-done((f32[5,4,32,128]{3,2,1,0:T(8,128)S(1)}, f32[5,4,32,128]{3,2,1,0:T(8,128)}, u32[]{:S(2)}) %copy-start) | copy-done | bytes 327704
  1.7 0.0 copy-start.1
  1.7 0.7 %copy-done.1 = f32[32,128]{1,0:T(8,128)S(1)} copy-done((f32[32,128]{1,0:T(8,128)S(1)}, f32[32,128]{1,0:T(8,128)}, u32[]{:S(2)}) %copy-start.1) | copy-done | bytes 16408
  2.4 0.0 copy-start.2
  2.4 0.7 %copy-done.2 = s32[32,128]{1,0:T(8,128)S(1)} copy-done((s32[32,128]{1,0:T(8,128)S(1)}, s32[32,128]{1,0:T(8,128)}, u32[]{:S(2)}) %copy-start.2) | copy-done | bytes 16408
  3.1 0.0 copy-start.3
  3.1 0.7 %copy-done.3 = f32[4,5,4]{1,2,0:T(4,128)S(1)} copy-done((f32[4,5,4]{1,2,0:T(4,128)S(1)}, f32[4,5,4]{1,2,0:T(4,128)}, u32[]{:S(2)}) %copy-start.3) | copy-done | bytes 344
  3.8 0.0 copy-start.4
  3.8 0.7 %copy-done.4 = f32[4,5,4]{1,2,0:T(4,128)S(1)} copy-done((f32[4,5,4]{1,2,0:T(4,128)S(1)}, f32[4,5,4]{1,2,0:T(4,128)}, u32[]{:S(2)}) %copy-start.4) | copy-done | bytes 344
  4.5 31.1 %shard_map.64 = f32[5,4,32,128]{3,2,1,0:T(8,128)S(1)} custom-call(f32[5,4,32,128]{3,2,1,0:T(8,128)S(1)} %copy-done, f32[32,128]{1,0:T(8,128)S(1)} %copy-done.1, s32[32,128]{1,0:T(8,128)S(1)} %copy-done.2, f32[4,4,5]{2,1,0:T(4,128)S(1)} %bitcast.3, f32[4,4,5]{2,1,0:T(4,128)S(1)} %bitcast.4, s32[2,3]{1,0:T(2,128)S(1)} %bitcast.5), custom_call_target="tpu_custom_call" | custom-call | tf_op jit(solution)/shard_map/pallas_call | solution.py:687
  35.6 0.7 %copy.8 = f32[5,4,32,128]{3,2,1,0:T(8,128)} copy(f32[5,4,32,128]{3,2,1,0:T(8,128)S(1)} %shard_map.64) | data formatting | bytes 655360
Async XLA Ops:
  0.0 0.7 %copy-start.5 = (s32[3,2]{0,1:T(2,128)S(1)}, s32[3,2]{0,1:T(2,128)}, u32[]{:S(2)}) copy-start(s32[3,2]{0,1:T(2,128)} %param.11) | copy-start | bytes 76
  0.7 1.0 %copy-start = (f32[5,4,32,128]{3,2,1,0:T(8,128)S(1)}, f32[5,4,32,128]{3,2,1,0:T(8,128)}, u32[]{:S(2)}) copy-start(f32[5,4,32,128]{3,2,1,0:T(8,128)} %whole.1) | copy-start | bytes 983044
  1.7 0.7 %copy-start.1 = (f32[32,128]{1,0:T(8,128)S(1)}, f32[32,128]{1,0:T(8,128)}, u32[]{:S(2)}) copy-start(f32[32,128]{1,0:T(8,128)} %mix.1) | copy-start | bytes 49156
  2.4 0.7 %copy-start.2 = (s32[32,128]{1,0:T(8,128)S(1)}, s32[32,128]{1,0:T(8,128)}, u32[]{:S(2)}) copy-start(s32[32,128]{1,0:T(8,128)} %mask.1) | copy-start | bytes 49156
  3.1 0.7 %copy-start.3 = (f32[4,5,4]{1,2,0:T(4,128)S(1)}, f32[4,5,4]{1,2,0:T(4,128)}, u32[]{:S(2)}) copy-start(f32[4,5,4]{1,2,0:T(4,128)} %param.9) | copy-start | bytes 964
  3.8 0.7 %copy-start.4 = (f32[4,5,4]{1,2,0:T(4,128)S(1)}, f32[4,5,4]{1,2,0:T(4,128)}, u32[]{:S(2)}) copy-start(f32[4,5,4]{1,2,0:T(4,128)} %param.10) | copy-start | bytes 964

commit v2 on v1

--- a/solution.py
+++ b/solution.py
@@ -29,13 +29,18 @@
     row_tiles,
     col_tiles,
     whole,
+    mix_in,
+    mask_in,
+    nu_in,
+    adv_in,
+    anchors_in,
+    out,
+    state,
     mix,
     mask,
     nu,
     adv,
     anchors,
-    out,
-    state,
     current,
     packs,
     held,
@@ -103,8 +108,21 @@
             device_id_type=MESH,
         )
 
-    fetch = pltpu.make_async_copy(whole, state, load_sem)
-    fetch.start()
+    loads = [
+        pltpu.make_async_copy(source, target, load_sem.at[index])
+        for index, (source, target) in enumerate(
+            (
+                (whole, state),
+                (mix_in, mix),
+                (mask_in, mask),
+                (nu_in, nu),
+                (adv_in, adv),
+                (anchors_in, anchors),
+            )
+        )
+    ]
+    for load in loads:
+        load.start()
     barrier = pltpu.get_barrier_semaphore()
 
     def greet(target):
@@ -300,11 +318,13 @@
 
     at_row_end = (i == 0) | (i == half_rows - 1)
     at_col_end = (j == 0) | (j == col_tiles - 1)
-    number_here = jnp.maximum(domain - 1, 0)
-    row_here = anchors[0, number_here] // nrow
-    col_here = anchors[1, number_here] // ncol
-    option_here = jnp.where(domain == 1, row_here - 1, row_here // foot)
-    slot_here = jnp.clip(option_here * places + col_here, 0, old_rows.shape[0] - 1)
+    def find_slot():
+        number_here = jnp.maximum(domain - 1, 0)
+        row_here = anchors[0, number_here] // nrow
+        col_here = anchors[1, number_here] // ncol
+        option_here = jnp.where(domain == 1, row_here - 1, row_here // foot)
+        slot = option_here * places + col_here
+        return row_here, jnp.clip(slot, 0, old_rows.shape[0] - 1)
 
     def edges_in(phase):
         def wait(slot):
@@ -337,6 +357,8 @@
         @pl.when(domain > 1)
         def _():
             repeat(2 * places, wait)
+
+        row_here, slot_here = find_slot()
 
         @pl.when(at_row_end)
         def _():
@@ -436,6 +458,8 @@
     def get(buffer, *prefix):
         return lambda f, level: buffer[(*prefix, f, level)]
 
+    for load in loads[1:]:
+        load.wait()
     mixing = mix[...]
     ratio = None
     for level in range(nlevel):
@@ -448,7 +472,7 @@
         coef[level] = inverse
         coef[nlevel + level] = ratio
 
-    fetch.wait()
+    loads[0].wait()
     pack(get(state), 0)
     backs = jnp.minimum(span - 1, j) - jnp.maximum(0, j - span) + 1
     gaps = jnp.minimum(foot - 1, i - 1) - jnp.maximum(0, i - foot) + 1
@@ -568,7 +592,7 @@
         def _():
             swap().start()
             swap().wait_recv()
-            mine = row_here == parity * foot
+            mine = find_slot()[0] == parity * foot
             chosen[...] = jnp.where(mine, piece[...], swapped[...])
             repeat(places, lambda place: feed_slot(place).start())
 
@@ -682,15 +706,19 @@
     sent = 4 * foot * span
     f32 = jnp.float32
     vmem = pl.BlockSpec(memory_space=pltpu.VMEM)
-    smem = pl.BlockSpec(memory_space=pltpu.SMEM)
     dma = pltpu.SemaphoreType.DMA
     return pl.pallas_call(
         functools.partial(kernel, row_tiles, col_tiles),
         out_shape=jax.ShapeDtypeStruct(state.shape, f32),
-        in_specs=[pl.BlockSpec(memory_space=pltpu.HBM), vmem, vmem, smem, smem, smem],
+        in_specs=[pl.BlockSpec(memory_space=pl.ANY)] * 6,
         out_specs=vmem,
         scratch_shapes=[
             pltpu.VMEM(state.shape, f32),
+            pltpu.VMEM((nrow, ncol), f32),
+            pltpu.VMEM((nrow, ncol), jnp.int32),
+            pltpu.SMEM((4, nlevel, nfield), f32),
+            pltpu.SMEM((4, nlevel, nfield), f32),
+            pltpu.SMEM((2, 3), jnp.int32),
             pltpu.VMEM((2, nfield, nlevel, nrow, ncol), f32),
             pltpu.VMEM((3, 2 * padded + nrow, ncol), f32),
             pltpu.VMEM((2, 2 * padded + nrow, ncol), f32),
@@ -710,7 +738,7 @@
             pltpu.VMEM((tall, ncol), f32),
             pltpu.VMEM((foot * places, 4, tall, ncol), f32),
             pltpu.VMEM((places, 4, tall, ncol), f32),
-            dma,
+            dma((6,)),
             dma((3, 4)),
             dma((3, 4)),
             dma((2, 3)),
@@ -725,14 +753,14 @@
         compiler_params=pltpu.CompilerParams(
             has_side_effects=True, collective_id=0, vmem_limit_bytes=VMEM_LIMIT
         ),
-    )(
+    )(*[pltpu.with_memory_space_constraint(v, pltpu.HBM) for v in (
         state,
         vert_mix,
         fb_mask,
         jnp.swapaxes(nu_coef, 1, 2),
         jnp.swapaxes(adv_coef, 1, 2),
         jnp.swapaxes(anchors, 0, 1),
-    )
+    )])
 
 
 def solution(mesh):

time: 37 us -> 31.4 us (0.85)
  local copies, waits for them, and re-layouts: 5.2 us -> 0.73 us
  Pallas kernels: 31.1 us -> 30.2 us
    unnamed x13 -> x1, local copies, waits for them, and re-layouts: 5.2 us -> 0.73 us
    pallas_call x1, Pallas kernels: 31.1 us -> 30.2 us  [shards(): pl.pallas_call(functools.partial(kernel, row_tiles, col_tiles), out_shape...]
where the time goes in v2:
time: 31.4 us; the launch traced here: 31 us
  Pallas kernels  30.2 us (96%)
  local copies, waits for them, and re-layouts  0.73 us (2%)
    pallas_call x1, Pallas kernels, shards(): pl.pallas_call(functools.partial(kernel, row_tiles, col_tiles), out_shape...  30.2 us
    unnamed x1, local copies, waits for them, and re-layouts  0.73 us

profile of v2, /device:TPU:8, one launch (start us, length us, event | category | flops | bytes accessed | tf_op | source)
XLA Modules:
  0.0 31.0 jit_solution(12359979437669567398)
XLA Ops:
  0.0 30.2 %shard_map.64 = f32[5,4,32,128]{3,2,1,0:T(8,128)S(1)} custom-call(f32[5,4,32,128]{3,2,1,0:T(8,128)} %whole.1, f32[32,128]{1,0:T(8,128)} %mix_in.1, s32[32,128]{1,0:T(8,128)} %mask_in.1, f32[4,4,5]{2,1,0:T(4,128)} %bitcast.3, f32[4,4,5]{2,1,0:T(4,128)} %bitcast.4, s32[2,3]{1,0:T(2,128)} %bitcast.5), custom_call_target="tpu_custom_call" | custom-call | tf_op jit(solution)/shard_map/pallas_call | solution.py:710
  30.3 0.7 %copy.8 = f32[5,4,32,128]{3,2,1,0:T(8,128)} copy(f32[5,4,32,128]{3,2,1,0:T(8,128)S(1)} %shard_map.64) | data formatting | bytes 655360

commit v3 on v2

--- a/solution.py
+++ b/solution.py
@@ -44,6 +44,8 @@
     current,
     packs,
     held,
+    side_packs,
+    side_halos,
     halo_rows,
     halo_cols,
     old_rows,
@@ -63,6 +65,8 @@
     load_sem,
     halo_send,
     halo_recv,
+    group_send,
+    group_recv,
     tell_send,
     held_recv,
     edge_send,
@@ -204,6 +208,57 @@
             packs[phase, padded + count : 2 * padded, :] = rest
         packs[phase, 2 * padded :, :] = packed
 
+    split = 2
+    groups = (range(split), range(split, nfield))
+    spans = ((0, split * nlevel), (split * nlevel, padded - split * nlevel))
+
+    def pack_group(load, phase, g):
+        packed = jnp.zeros((nrow, ncol), jnp.float32)
+        for f in groups[g]:
+            for level in range(nlevel):
+                k = f * nlevel + level
+                cells = load(f, level)
+                packs[phase, k : k + 1, :] = cells[0:1, :]
+                packs[phase, padded + k : padded + k + 1, :] = cells[nrow - 1 : nrow, :]
+                rolled = pltpu.roll(cells, 2 * k + 1, 1)
+                packed = jnp.where((lane == 2 * k) | (lane == 2 * k + 1), rolled, packed)
+        if g == 1 and padded > count:
+            rest = jnp.zeros((padded - count, ncol), jnp.float32)
+            packs[phase, count:padded, :] = rest
+            packs[phase, padded + count : 2 * padded, :] = rest
+        side_packs[phase - 1, g] = packed
+
+    def halo_group(phase, g, act):
+        start, size = spans[g]
+        top, low = pl.ds(start, size), pl.ds(padded + start, size)
+        down, up = i < half_rows - 1, i > 0
+        right, left = j < col_tiles - 1, j > 0
+        moves = (
+            (0, down, packs.at[phase, low], halo_rows.at[phase, 0, top], i + 1, j, up),
+            (1, up, packs.at[phase, top], halo_rows.at[phase, 1, top], i - 1, j, down),
+            (2, right, side_packs.at[phase - 1, g], side_halos.at[phase - 1, g, 0], i, j + 1, left),
+            (3, left, side_packs.at[phase - 1, g], side_halos.at[phase - 1, g, 1], i, j - 1, right),
+        )
+        for way, sends, source, dest, row, col, takes in moves:
+
+            def go(source=source, dest=dest, row=row, col=col, way=way):
+                return copy(
+                    source,
+                    dest,
+                    group_send.at[phase - 1, g, way],
+                    group_recv.at[phase - 1, g, way],
+                    device(domain, row, col),
+                )
+
+            @pl.when(takes if act == "recv" else sends)
+            def _():
+                if act == "start":
+                    go().start()
+                elif act == "recv":
+                    go().wait_recv()
+                else:
+                    go().wait_send()
+
     first_row = pl.ds(0, padded)
     last_row = pl.ds(padded, padded)
     side_cols = pl.ds(2 * padded, nrow)
@@ -378,11 +433,38 @@
             spread_cols[phase, pl.ds(0, hrow, stride=2), :] = values
             spread_cols[phase, pl.ds(1, hrow, stride=2), :] = values
 
+    def ghosts_group(phase, g):
+        start, size = spans[g]
+        rows = slice(start, start + size)
+        weight = phase / SUBSTEPS
+        for side, inner in ((0, i > 0), (1, i < half_rows - 1)):
+
+            @pl.when(inner)
+            def _():
+                ghost_rows[side, rows, :] = halo_rows[phase, side, rows, :]
+
+            @pl.when(jnp.logical_not(inner))
+            def _():
+                old, new = spread_rows[0, rows, :], spread_rows[1, rows, :]
+                ghost_rows[side, rows, :] = old + weight * (new - old)
+
+        for side, inner in ((0, j > 0), (1, j < col_tiles - 1)):
+
+            @pl.when(inner)
+            def _():
+                ghost_cols[side] = side_halos[phase - 1, g, side]
+
+            if g == 0:
+
+                @pl.when(jnp.logical_not(inner))
+                def _():
+                    shift = ncol - 1 if side == 0 else 1
+                    old, new = spread_cols[0], spread_cols[1]
+                    ghost_cols[side] = pltpu.roll(old + weight * (new - old), shift, 1)
+
     def ghosts(phase):
         def blended(values):
-            if phase == 0:
-                return values[0]
-            return values[0] + (phase / SUBSTEPS) * (values[1] - values[0])
+            return values[0]
 
         for side, inner in ((0, i > 0), (1, i < half_rows - 1)):
 
@@ -413,10 +495,10 @@
             def _():
                 ghost_cols[side] = jnp.zeros((nrow, ncol), jnp.float32)
 
-    def advance(load, store):
+    def advance(load, store, fields=range(nfield)):
         sides = jnp.where(lane % 2 == 0, ghost_cols[0], ghost_cols[1])
         mixing = mix[...]
-        for f in range(nfield):
+        for f in fields:
             forward = []
             for level in range(nlevel):
                 k = f * nlevel + level
@@ -491,7 +573,7 @@
 
     @pl.when(is_parent)
     def _():
-        for number in (1, 2, 3):
+        for number in (2, 3, 1):
             tell(0, number).start()
 
     halo(0, "start")
@@ -508,99 +590,141 @@
         edges_in(0)
 
     ghosts(0)
-    advance(get(state), put(current, 0))
-    pack(get(current, 0), 1)
+
+    @pl.when(is_nest)
+    def _():
+        for g in range(2):
+            advance(get(state), put(current, 0), groups[g])
+            pack_group(get(current, 0), 1, g)
+            halo_group(1, g, "start")
 
     @pl.when(is_parent)
     def _():
-        for number in (1, 2, 3):
+        advance(get(state), put(current, 0))
+        pack(get(current, 0), 1)
+        for number in (2, 3, 1):
             tell(1, number).start()
 
     feeds = foot * places
-
-    def feed_one(flat):
+    home = j - j // 2
+
+    def far_first(step):
+        down = (home - 1 - step + places) % places
+        return jnp.where(j < span, down, (home + 1 + step) % places)
+
+    def cut_of(ref, chunk):
+        return ref.at[pl.ds(0, half * hrow) if chunk == 0 else pl.ds(half * hrow, hrow)]
+
+    def feed_one(flat, chunk):
         option = flat // places
         place = flat % places
         where_to = device(0, 1 + option + i // 2, place + j // 2)
         part = 2 * (i % 2) + j % 2
         return copy(
-            chosen,
-            one_sums.at[flat, part],
-            feed_send.at[flat],
-            one_recv.at[flat, part],
+            cut_of(piece, chunk),
+            cut_of(one_sums.at[flat, part], chunk),
+            feed_send.at[chunk, flat],
+            one_recv.at[chunk, flat, part],
             where_to,
         )
 
-    def feed_slot(place):
+    def feed_ones(chunk):
+        repeat(
+            feeds,
+            lambda step: feed_one(step // places * places + far_first(step % places), chunk).start(),
+        )
+
+    def feed_slot(place, chunk):
         where_to = device(0, parity * foot + i // 2, place + j // 2)
         part = 2 * (i % 2) + j % 2
         return copy(
-            chosen,
-            slot_sums.at[place, part],
-            feed_send.at[place],
-            slot_recv.at[place, part],
+            cut_of(chosen, chunk),
+            cut_of(slot_sums.at[place, part], chunk),
+            feed_send.at[chunk, place],
+            slot_recv.at[chunk, place, part],
             where_to,
         )
 
-    def swap():
+    def swap(chunk):
         return copy(
-            piece, swapped, swap_sem.at[0], swap_sem.at[1], (dom, 2 * i + 1 - parity, j)
+            cut_of(piece, chunk),
+            cut_of(swapped, chunk),
+            swap_sem.at[chunk, 0],
+            swap_sem.at[chunk, 1],
+            (dom, 2 * i + 1 - parity, j),
         )
 
+    def feed_slots(chunk):
+        mine = find_slot()[0] == parity * foot
+        swap(chunk).wait_recv()
+        part = cut_of(chosen, chunk)
+        part[...] = jnp.where(mine, cut_of(piece, chunk)[...], cut_of(swapped, chunk)[...])
+        repeat(places, lambda step: feed_slot(far_first(step), chunk).start())
+
     @pl.when(is_nest)
     def _():
-        halo(1, "start")
-        halo(1, "recv")
-        edges_in(1)
-        ghosts(1)
-        advance(get(current, 0), put(current, 1))
-        pack(get(current, 1), 2)
-        halo(2, "start")
-        halo(2, "recv")
-        ghosts(2)
-        advance(get(current, 1), put(out))
         source = lax.broadcasted_iota(jnp.int32, (2 * ncol, ncol), 0)
         target = lax.broadcasted_iota(jnp.int32, (2 * ncol, ncol), 1)
         gather = (target == source // 2).astype(jnp.float32)
         even = mask[pl.ds(0, hrow, stride=2), :].astype(jnp.float32)
         odd = mask[pl.ds(1, hrow, stride=2), :].astype(jnp.float32)
 
-        def pairs(k):
+        def offer(chunk, blocks):
+            part = cut_of(piece, chunk)
+            part[...] = jnp.dot(
+                jnp.concatenate(blocks, axis=0),
+                gather,
+                precision=lax.Precision.HIGHEST,
+                preferred_element_type=jnp.float32,
+            )
+
+            @pl.when(domain == 1)
+            def _():
+                feed_ones(chunk)
+
+            @pl.when(domain > 1)
+            def _():
+                swap(chunk).start()
+
+        offer(1, [jnp.concatenate([even + odd, jnp.zeros_like(even)], axis=1)])
+        edges_in(1)
+        for g in range(2):
+            halo_group(1, g, "recv")
+            ghosts_group(1, g)
+            advance(get(current, 0), put(current, 1), groups[g])
+            pack_group(get(current, 1), 2, g)
+            halo_group(2, g, "start")
+
+        @pl.when(domain > 1)
+        def _():
+            feed_slots(1)
+
+        for g in range(2):
+            halo_group(2, g, "recv")
+            ghosts_group(2, g)
+            advance(get(current, 1), put(out), groups[g])
+
+        def weighed(k):
             f, level = k // nlevel, k % nlevel
             return (
                 even * out[f, level, pl.ds(0, hrow, stride=2), :]
                 + odd * out[f, level, pl.ds(1, hrow, stride=2), :]
             )
 
-        tall = []
-        for k in range(half):
-            tall.append(jnp.concatenate([pairs(k), pairs(k + half)], axis=1))
-        tall.append(jnp.concatenate([even + odd, jnp.zeros_like(even)], axis=1))
-        piece[...] = jnp.dot(
-            jnp.concatenate(tall, axis=0),
-            gather,
-            precision=lax.Precision.HIGHEST,
-            preferred_element_type=jnp.float32,
+        offer(
+            0,
+            [jnp.concatenate([weighed(k), weighed(k + half)], axis=1) for k in range(half)],
         )
 
-        @pl.when(domain == 1)
-        def _():
-            chosen[...] = piece[...]
-            repeat(feeds, lambda flat: feed_one(flat).start())
-
         @pl.when(domain > 1)
         def _():
-            swap().start()
-            swap().wait_recv()
-            mine = find_slot()[0] == parity * foot
-            chosen[...] = jnp.where(mine, piece[...], swapped[...])
-            repeat(places, lambda place: feed_slot(place).start())
+            feed_slots(0)
 
     @pl.when(is_parent)
     def _():
         away = device(1, i // 2, j // 2)
 
-        def take_one(flat):
+        def take_one(flat, chunk):
             option = flat // places
             place = flat % places
             row_gap = i - 1 - option
@@ -610,29 +734,30 @@
             def _():
                 for part in range(4):
                     copy(
-                        chosen,
-                        one_sums.at[flat, part],
-                        feed_send.at[0],
-                        one_recv.at[flat, part],
+                        cut_of(piece, chunk),
+                        cut_of(one_sums.at[flat, part], chunk),
+                        feed_send.at[chunk, 0],
+                        one_recv.at[chunk, flat, part],
                         away,
                     ).wait_recv()
 
-        def take_slot(place):
+        def take_slot(place, chunk):
             back = j - place
 
             @pl.when((back >= 0) & (back < span))
             def _():
                 for part in range(4):
                     copy(
-                        chosen,
-                        slot_sums.at[place, part],
-                        feed_send.at[0],
-                        slot_recv.at[place, part],
+                        cut_of(chosen, chunk),
+                        cut_of(slot_sums.at[place, part], chunk),
+                        feed_send.at[chunk, 0],
+                        slot_recv.at[chunk, place, part],
                         away,
                     ).wait_recv()
 
-        repeat(feeds, take_one)
-        repeat(places, take_slot)
+        for chunk in (1, 0):
+            repeat(feeds, lambda flat: take_one(flat, chunk))
+            repeat(places, lambda place: take_slot(place, chunk))
         one_row = anchors[0, 0] // nrow
         one_col = anchors[1, 0] // ncol
         slot = i // foot
@@ -679,19 +804,22 @@
 
     @pl.when(is_nest)
     def _():
-        halo(1, "send")
-        halo(2, "send")
+        for g in range(2):
+            halo_group(1, g, "send")
+            halo_group(2, g, "send")
         edges_out(0, "send")
         edges_out(1, "send")
 
         @pl.when(domain == 1)
         def _():
-            repeat(feeds, lambda flat: feed_one(flat).wait_send())
+            for chunk in range(2):
+                repeat(feeds, lambda flat: feed_one(flat, chunk).wait_send())
 
         @pl.when(domain > 1)
         def _():
-            swap().wait_send()
-            repeat(places, lambda place: feed_slot(place).wait_send())
+            for chunk in range(2):
+                swap(chunk).wait_send()
+                repeat(places, lambda place: feed_slot(place, chunk).wait_send())
 
 
 def shards(row_tiles, col_tiles, state, vert_mix, fb_mask, nu_coef, adv_coef, anchors):
@@ -722,8 +850,10 @@
             pltpu.VMEM((2, nfield, nlevel, nrow, ncol), f32),
             pltpu.VMEM((3, 2 * padded + nrow, ncol), f32),
             pltpu.VMEM((2, 2 * padded + nrow, ncol), f32),
+            pltpu.VMEM((2, 2, nrow, ncol), f32),
+            pltpu.VMEM((2, 2, 2, nrow, ncol), f32),
             pltpu.VMEM((3, 2, padded, ncol), f32),
-            pltpu.VMEM((3, 2, nrow, ncol), f32),
+            pltpu.VMEM((1, 2, nrow, ncol), f32),
             pltpu.VMEM((options * places, padded, ncol), f32),
             pltpu.VMEM((options * places, padded, ncol), f32),
             pltpu.VMEM((options * places, nrow // 2, ncol), f32),
@@ -739,16 +869,18 @@
             pltpu.VMEM((foot * places, 4, tall, ncol), f32),
             pltpu.VMEM((places, 4, tall, ncol), f32),
             dma((6,)),
-            dma((3, 4)),
-            dma((3, 4)),
+            dma((1, 4)),
+            dma((1, 4)),
+            dma((2, 2, 4)),
+            dma((2, 2, 4)),
             dma((2, 3)),
             dma((2,)),
             dma((2, 2, sent)),
             dma((2, 2, options * places)),
-            dma((2,)),
-            dma((foot * places,)),
-            dma((foot * places, 4)),
-            dma((places, 4)),
+            dma((2, 2)),
+            dma((2, foot * places)),
+            dma((2, foot * places, 4)),
+            dma((2, places, 4)),
         ],
         compiler_params=pltpu.CompilerParams(
             has_side_effects=True, collective_id=0, vmem_limit_bytes=VMEM_LIMIT

time: 31.4 us -> 30.5 us (0.971); the launches traced: 31 us -> 30.4 us
  Pallas kernels: 30.2 us -> 29.7 us
    pallas_call x1, Pallas kernels: 30.2 us -> 29.7 us  [shards(): pl.pallas_call(functools.partial(kernel, row_tiles, col_tiles), out_shape...]
where the time goes in v3:
time: 30.5 us; the launch traced here: 30.4 us
  Pallas kernels  29.7 us (97%)
  local copies, waits for them, and re-layouts  0.73 us (2%)
    pallas_call x1, Pallas kernels, shards(): pl.pallas_call(functools.partial(kernel, row_tiles, col_tiles), out_shape...  29.7 us
    unnamed x1, local copies, waits for them, and re-layouts  0.73 us

profile of v3, /device:TPU:8, one launch (start us, length us, event | category | flops | bytes accessed | tf_op | source)
XLA Modules:
  0.0 30.4 jit_solution(9823823404933662587)
XLA Ops:
  0.0 29.7 %shard_map.64 = f32[5,4,32,128]{3,2,1,0:T(8,128)S(1)} custom-call(f32[5,4,32,128]{3,2,1,0:T(8,128)} %whole.1, f32[32,128]{1,0:T(8,128)} %mix_in.1, s32[32,128]{1,0:T(8,128)} %mask_in.1, f32[4,4,5]{2,1,0:T(4,128)} %bitcast.3, f32[4,4,5]{2,1,0:T(4,128)} %bitcast.4, s32[2,3]{1,0:T(2,128)} %bitcast.5), custom_call_target="tpu_custom_call" | custom-call | tf_op jit(solution)/shard_map/pallas_call | solution.py:838
  29.7 0.7 %copy.8 = f32[5,4,32,128]{3,2,1,0:T(8,128)} copy(f32[5,4,32,128]{3,2,1,0:T(8,128)S(1)} %shard_map.64) | data formatting | bytes 655360
